TPU v7x, 256 devices: a whole 4x4x8 slice. The times are simulated.
256 devices in a mesh: req: 64 (over x, z, core), tp: 4 (over y).
Axes of the slice: x: 4, y: 4, z: 8, core: 2. Of those that a mesh axis runs over, the one named last changes fastest.
Arguments:
- attn_values: bfloat16 [16384, 2048], P('req', 'tp'), may hold values from -0.5 to 0.5
- out_proj: bfloat16 [2048, 2048], P('tp'), may hold values from -0.125 to 0.125
- residual_in: bfloat16 [16384, 2048], P(('req', 'tp')), may hold values from -0.5 to 0.5
- norm_gain: bfloat16 [2048], replicated, may hold values from 0.099609375 to 1.8984375
- final_gain: bfloat16 [2048], replicated, may hold values from 0.099609375 to 1.8984375
- router: bfloat16 [2048, 8], replicated, may hold values from -0.03125 to 0.03125
- gate_weight: bfloat16 [64, 2048, 640], P('req'), may hold values from -0.125 to 0.125
- up_weight: bfloat16 [64, 2048, 640], P('req'), may hold values from -0.125 to 0.125
- down_weight: bfloat16 [64, 640, 2048], P('req'), may hold values from -2 to 2
- row_order: int32 [16384], P(('req', 'tp')), may hold values from 0 to 16383, as said below
- routes: int32 [16384, 2], P(('req', 'tp')), may hold values from 0 to 7, all different within a row; in each aligned block of 64 rows (0 to 63, 64 to 127, ...) at most 32 rows name the same one
Outputs:
- layer_out: bfloat16 [16384, 2048], P(('req', 'tp'))
Inputs may be any that keep to these rules, and one draw needn't show every extreme that they name: row_order permutes each aligned block of 64 positions within itself. `routes`: in each aligned block of 64 rows (the rows of one device) a row names two different experts and no expert is named more than 32 times; in every draw some expert is named exactly 32 times in some block.
All inputs are finite; a program needn't handle non-finite values.
Results may differ from a plain program's by a relative error of at most 0.01.
Values may be sent and summed in bfloat16 or wider, within the bound.
A program may use at most 128 MiB of HBM per device.

v0:
```python
import jax
import jax.numpy as jnp
from jax import lax
from jax.sharding import PartitionSpec as P

TOP = 2
CAP = 32


def root_norm(values, scale_gain):
    mean_sq = jnp.mean(values * values, axis=-1, keepdims=True)
    return values * lax.rsqrt(mean_sq + 1e-06) * scale_gain.astype(jnp.float32)


def shards(
    attn_values,
    out_proj,
    residual_in,
    norm_gain,
    final_gain,
    router,
    gate_weight,
    up_weight,
    down_weight,
    row_order,
    routes,
):
    row_count = residual_in.shape[0]
    width = residual_in.shape[1]
    tp_count = lax.axis_size("tp")
    req_count = lax.axis_size("req")
    experts = router.shape[1]
    holders = req_count // experts
    my_index = lax.axis_index("req")
    attn_out = lax.psum_scatter(
        jnp.dot(attn_values, out_proj, preferred_element_type=jnp.float32),
        "tp",
        scatter_dimension=0,
        tiled=True,
    )
    stream = (residual_in.astype(jnp.float32) + attn_out).astype(jnp.bfloat16)
    normed = root_norm(stream.astype(jnp.float32), norm_gain).astype(jnp.bfloat16)
    block_start = (my_index * tp_count + lax.axis_index("tp")) * row_count
    local_order = row_order - block_start
    picked = jnp.take(normed, local_order, axis=0)
    kept = jnp.take(stream, local_order, axis=0).astype(jnp.float32)
    logits = jnp.dot(picked, router, preferred_element_type=jnp.float32)
    onehot = (routes[:, :, None] == jnp.arange(experts, dtype=jnp.int32)[None, None, :]).astype(
        jnp.int32
    )
    chosen = jnp.sum(logits[:, None, :] * onehot.astype(jnp.float32), axis=-1)
    weight_a = jax.nn.sigmoid(chosen[:, 0] - chosen[:, 1])
    weight_b = jax.nn.sigmoid(chosen[:, 1] - chosen[:, 0])
    flat_hot = onehot.reshape(row_count * TOP, experts)
    before = jnp.cumsum(flat_hot, axis=0) - flat_hot
    slot_rank = jnp.sum(before * flat_hot, axis=-1).reshape(row_count, TOP)
    position = routes * CAP + slot_rank
    slot_table = (
        position[:, :, None] == jnp.arange(experts * CAP, dtype=jnp.int32)[None, None, :]
    ).astype(jnp.float32)
    dispatch = jnp.sum(slot_table, axis=1).astype(jnp.bfloat16)
    pair_w = jnp.stack([weight_a, weight_b], axis=1)
    combine_w = jnp.sum(slot_table * pair_w[:, :, None], axis=1)
    send_rows = jnp.einsum(
        "rc,rd->cd", dispatch, picked, preferred_element_type=jnp.float32
    ).astype(jnp.bfloat16)
    copies = jnp.broadcast_to(
        send_rows.reshape(experts, 1, CAP, width), (experts, holders, CAP, width)
    )
    copies = copies.reshape(req_count, CAP, width)
    item_rows = lax.all_to_all(copies, "req", split_axis=0, concat_axis=0, tiled=True)
    count = item_rows.shape[1]
    flat_rows = item_rows.reshape(-1, width)
    gate_val = jnp.dot(flat_rows, gate_weight[0], preferred_element_type=jnp.float32)
    up_val = jnp.dot(flat_rows, up_weight[0], preferred_element_type=jnp.float32)
    hidden = (jax.nn.silu(gate_val) * up_val).astype(jnp.bfloat16)
    partial_value = jnp.dot(hidden, down_weight[0], preferred_element_type=jnp.float32)
    partial_value = partial_value.reshape(item_rows.shape[0], count, width)
    returned = lax.all_to_all(partial_value, "req", split_axis=0, concat_axis=0, tiled=True)
    expert_out = jnp.sum(returned.reshape(experts, holders, CAP, width), axis=1)
    moe = jnp.dot(
        combine_w,
        expert_out.reshape(experts * CAP, width),
        precision=lax.Precision.HIGHEST,
        preferred_element_type=jnp.float32,
    )
    normed_out = root_norm(kept + moe, final_gain).astype(jnp.bfloat16)
    return jnp.zeros((row_count, width), jnp.bfloat16).at[local_order].set(normed_out)


def solution(mesh):
    placed = (
        P("req", "tp"),
        P("tp", None),
        P(("req", "tp"), None),
        P(),
        P(),
        P(),
        P("req", None, None),
        P("req", None, None),
        P("req", None, None),
        P(("req", "tp")),
        P(("req", "tp"), None),
    )
    return jax.shard_map(
        shards, mesh=mesh, in_specs=placed, out_specs=P(("req", "tp"), None), check_vma=False
    )
```

profile of v0, /device:TPU:10, one launch (start us, length us, event | category | flops | bytes accessed | tf_op | source)
XLA Modules:
  0.0 661.8 jit_solution(11953066012608031340)
XLA Ops:
  6.5 0.0 copy-start
  6.5 0.0 reduce-scatter.2.cloned.1.call-start
  6.6 3.9 fusion.17
  10.5 0.0 reduce-scatter.2.cloned.1.call-update
  10.5 0.0 copy-start.9
  10.5 0.1 copy.32
  10.6 0.1 eq.35
  10.8 0.1 fusion.13
  10.9 0.2 reduce_window_sum.11
  11.0 0.2 select_reduce_fusion.1
  11.2 0.1 reshape.49
  11.4 0.1 copy.33
  11.4 0.0 copy-done.6
  11.5 33.0 %reduce-scatter.2.cloned.1.call-done = f32[64,2048]{1,0:T(8,128)} async-done(((f32[256,2048]{1,0:T(8,128)}), f32[64,2048]{1,0:T(8,128)}) %reduce-scatter.2.cloned.1.call-update) | async-done | bytes 524304 | tf_op jit(solution)/shard_map/reduce_scatter | solution.py:35
  44.5 1.2 fusion.5
  45.8 0.1 fusion.7
  45.9 0.7 gather_fusion.1
  46.7 0.2 fusion.12
  47.0 0.1 convert_reduce_fusion
  47.1 0.5 convolution_convert_fusion
  47.6 1.1 broadcast_in_dim.20
  48.6 0.0 copy-start.7
  48.7 194.8 %all_to_all.10 = bf16[64,32,2048]{2,1,0:T(8,128)(2,1)S(1)} all-to-all(bf16[64,32,2048]{2,1,0:T(8,128)(2,1)S(1)} %bitcast.26), channel_id=1, replica_groups=mesh['req'=64,'tp'=4] {'req'}, dimensions={0} | all-to-all | bytes 16777216 | tf_op jit(solution)/shard_map/all_to_all | solution.py:71
  243.5 6.8 %fusion.3 = f32[2048,640]{1,0:T(8,128)S(1)} fusion(bf16[2048,2048]{1,0:T(8,128)(2,1)S(1)} %bitcast.28, bf16[1,2048,640]{2,1,0:T(8,128)(2,1)S(1)} %copy-done.7), kind=kOutput, calls=%fused_computation.8 | convolution fusion | flops 5368709120 | bytes 16252928 | tf_op jit(solution)/shard_map/dot_general | solution.py:74
  250.4 7.1 %multiply_convert_fusion = bf16[2048,640]{1,0:T(8,128)(2,1)S(1)} fusion(f32[2048,640]{1,0:T(8,128)S(1)} %fusion.3, bf16[2048,2048]{1,0:T(8,128)(2,1)S(1)} %bitcast.29, bf16[1,2048,640]{2,1,0:T(8,128)(2,1)S(1)} %copy-done.8), kind=kOutput, calls=%fused_computation.4 | convolution fusion | flops 5376573440 | bytes 18874368 | tf_op jit(solution)/shard_map/dot_general | solution.py:75
  257.5 10.2 %fusion = f32[64,32,2048]{2,1,0:T(8,128)} fusion(bf16[64,32,640]{2,1,0:T(8,128)(2,1)S(1)} %bitcast.31, bf16[1,640,2048]{2,1,0:T(8,128)(2,1)S(1)} %copy-done), kind=kOutput, calls=%fused_computation.5 | convolution fusion | flops 5368709120 | bytes 22020096 | tf_op jit(solution)/shard_map/dot_general | solution.py:77
  267.7 7.8 %all-to-all-start.1 = ((f32[64,32,2048]{2,1,0:T(8,128)}), f32[64,32,2048]{2,1,0:T(8,128)}, u32[]{:S(2)}, u32[]{:S(2)}) async-start(f32[64,32,2048]{2,1,0:T(8,128)} %fusion), calls=%async_computation.2 | async-start | bytes 33554432 | tf_op jit(solution)/shard_map/all_to_all | solution.py:79
  275.5 0.7 gather_fusion
  276.3 364.6 %all-to-all-done.1 = f32[64,32,2048]{2,1,0:T(8,128)} async-done(((f32[64,32,2048]{2,1,0:T(8,128)}), f32[64,32,2048]{2,1,0:T(8,128)}, u32[]{:S(2)}, u32[]{:S(2)}) %all-to-all-start.1) | async-done | bytes 16777248 | tf_op jit(solution)/shard_map/all_to_all | solution.py:79
  640.9 9.2 %bitcast_reduce_fusion = f32[8,32,2048]{2,1,0:T(8,128)} fusion(f32[64,32,2048]{2,1,0:T(8,128)} %all-to-all-done.1), kind=kLoop, calls=%fused_computation.3 | loop fusion | flops 3670016 | bytes 18874368 | tf_op jit(solution)/shard_map/reduce_sum | solution.py:80
  650.1 3.1 multiply_reduce_fusion
  653.2 1.7 scatter_custom_fusion
  (26 shorter events, 0.1 us)
Async XLA Ops:
  6.5 250.9 %copy-start = (bf16[1,640,2048]{2,1,0:T(8,128)(2,1)S(1)}, bf16[1,640,2048]{2,1,0:T(8,128)(2,1)}, u32[]{:S(2)}) copy-start(bf16[1,640,2048]{2,1,0:T(8,128)(2,1)} %param.21) | copy-start | bytes 7864324
  6.5 4.0 copy-start.3
  6.5 4.9 copy-start.4
  6.5 4.9 copy-start.6
  6.5 38.0 %copy-start.2 = (bf16[64,2048]{1,0:T(8,128)(2,1)S(1)}, bf16[64,2048]{1,0:T(8,128)(2,1)}, u32[]{:S(2)}) copy-start(bf16[64,2048]{1,0:T(8,128)(2,1)} %param.15) | copy-start | bytes 786436
  6.5 38.0 %reduce-scatter.2.cloned.1.call-start = ((), (), s32[]{:S(2)}) async-start(), calls=%async_computation.3 | async-start | bytes 2621440 | tf_op jit(solution)/shard_map/reduce_scatter | solution.py:35
  10.5 36.1 %copy-start.9 = (bf16[2048,8]{0,1:T(8,128)(2,1)S(1)}, bf16[2048,8]{0,1:T(8,128)(2,1)}, u32[]{:S(2)}) copy-start(bf16[2048,8]{0,1:T(8,128)(2,1)} %param.18) | copy-start | bytes 98308
  48.6 194.9 %copy-start.7 = (bf16[1,2048,640]{2,1,0:T(8,128)(2,1)S(1)}, bf16[1,2048,640]{2,1,0:T(8,128)(2,1)}, u32[]{:S(2)}) copy-start(bf16[1,2048,640]{2,1,0:T(8,128)(2,1)} %param.19) | copy-start | bytes 7864324
  243.5 6.9 %copy-start.8 = (bf16[1,2048,640]{2,1,0:T(8,128)(2,1)S(1)}, bf16[1,2048,640]{2,1,0:T(8,128)(2,1)}, u32[]{:S(2)}) copy-start(bf16[1,2048,640]{2,1,0:T(8,128)(2,1)} %param.20) | copy-start | bytes 7864324
  267.7 7.9 %copy-start.5 = (bf16[2048]{0:T(1024)(128)(2,1)S(1)}, bf16[2048]{0:T(1024)(128)(2,1)}, u32[]{:S(2)}) copy-start(bf16[2048]{0:T(1024)(128)(2,1)} %param.17) | copy-start | bytes 12292
  267.7 373.2 %all-to-all-start.1 = ((f32[64,32,2048]{2,1,0:T(8,128)}), f32[64,32,2048]{2,1,0:T(8,128)}, u32[]{:S(2)}, u32[]{:S(2)}) async-start(f32[64,32,2048]{2,1,0:T(8,128)} %fusion), calls=%async_computation.2 | async-start | bytes 33554432 | tf_op jit(solution)/shard_map/all_to_all | solution.py:79
  640.9 14.0 %copy-start.1 = (bf16[1,640,2048]{2,1,0:T(8,128)(2,1)S(1)}, bf16[1,640,2048]{2,1,0:T(8,128)(2,1)}, u32[]{:S(2)}) copy-start(bf16[1,640,2048]{2,1,0:T(8,128)(2,1)} %param.21) | copy-start | bytes 7864324
Sparse Core Ops, SparseCore 0:
  10.6 33.8 reduce-scatter.1
where the time goes:
time: 665 us; the launch traced here: 662 us
  waiting for transfers between devices  398 us (60%)
  blocking collectives  195 us (29%)
  matrix products  31.8 us (5%)
  between operations  13.6 us (2%)
  other arithmetic  12.9 us (2%)
  starting transfers between devices  7.88 us (1%)
    all_to_all x1, waiting for transfers between devices, shards(): lax.all_to_all(partial_value, 'req', split_axis=0, concat_axis=0, tiled=T...  365 us
    all_to_all x1, blocking collectives, shards(): lax.all_to_all(copies, 'req', split_axis=0, concat_axis=0, tiled=True)  195 us
    reduce_scatter x1, waiting for transfers between devices, shards(): lax.psum_scatter(jnp.dot(attn_values, out_proj, preferred_element_type=jn...  33 us
  transfers between devices with their start and end apart: 2, of which 2 were waited for; matrix products, arithmetic and copies ran while one was open for 0% of the time, Pallas kernels for 0%

commit v1 on v0

v1 whole, which is shorter than its diff:
```python
import jax
import jax.numpy as jnp
from jax import lax
from jax.sharding import Mesh, PartitionSpec as P

TOP = 2
CAP = 32
X, Z, C = 4, 8, 2
META = 128


def root_norm(values, scale_gain):
    mean_sq = jnp.mean(values * values, axis=-1, keepdims=True)
    return values * lax.rsqrt(mean_sq + 1e-06) * scale_gain.astype(jnp.float32)


def shards(
    attn_values,
    out_proj,
    residual_in,
    norm_gain,
    final_gain,
    router,
    gate_weight,
    up_weight,
    down_weight,
    row_order,
    routes,
):
    rows, width = residual_in.shape
    experts = router.shape[1]
    f32, bf16 = jnp.float32, jnp.bfloat16
    half = lax.axis_index("z") // (Z // 2)

    swap = [(0, 1), (1, 0)]
    gates = [gate_weight[0], lax.ppermute(gate_weight, "c", swap)[0]]
    ups = [up_weight[0], lax.ppermute(up_weight, "c", swap)[0]]
    downs = [down_weight[0], lax.ppermute(down_weight, "c", swap)[0]]

    attn_out = lax.psum_scatter(
        jnp.dot(attn_values, out_proj, preferred_element_type=f32).astype(bf16),
        "tp",
        scatter_dimension=0,
        tiled=True,
    ).astype(f32)
    stream = (residual_in.astype(f32) + attn_out).astype(bf16)
    normed = root_norm(stream.astype(f32), norm_gain).astype(bf16)

    local_order = lax.rem(row_order, rows)
    pick = (local_order[:, None] == jnp.arange(rows, dtype=jnp.int32)[None, :]).astype(bf16)
    picked = jnp.dot(pick, normed, preferred_element_type=f32).astype(bf16)

    logits = jnp.dot(picked, router, preferred_element_type=f32)
    onehot = (routes[:, :, None] == jnp.arange(experts, dtype=jnp.int32)).astype(jnp.int32)
    chosen = jnp.sum(logits[:, None, :] * onehot.astype(f32), axis=-1)
    weight_a = jax.nn.sigmoid(chosen[:, 0] - chosen[:, 1])
    weight_b = jax.nn.sigmoid(chosen[:, 1] - chosen[:, 0])
    flat_hot = onehot.reshape(rows * TOP, experts)
    earlier = jnp.tri(rows * TOP, k=-1, dtype=bf16)
    before = jnp.dot(earlier, flat_hot.astype(bf16), preferred_element_type=f32)
    rank = jnp.sum(before * flat_hot.astype(f32), axis=-1).reshape(rows, TOP)
    slot = (routes % 2 * (experts // 2 * CAP) + routes // 2 * CAP).astype(f32) + rank
    pair_w = jnp.stack([weight_a, weight_b], axis=1)
    w_hi = pair_w.astype(bf16)
    w_lo = (pair_w - w_hi.astype(f32)).astype(bf16)
    meta = jnp.concatenate([slot.astype(bf16), w_hi, w_lo], axis=1)
    meta = jnp.pad(meta, ((0, 0), (0, META - meta.shape[1])))

    column = lax.all_gather(jnp.concatenate([picked, meta], axis=1), "z", axis=0)
    half_slots = X * CAP
    local = column[:, :, width : width + TOP].astype(f32) - (half * half_slots).astype(f32)
    at = jnp.arange(half_slots, dtype=f32)
    table = (local[:, :, :, None] == at).astype(bf16)
    dispatch = table[:, :, 0] + table[:, :, 1]
    w = column[:, :, width + TOP : width + 3 * TOP]
    comb_hi = table[:, :, 0] * w[:, :, 0:1] + table[:, :, 1] * w[:, :, 1:2]
    comb_lo = table[:, :, 0] * w[:, :, 2:3] + table[:, :, 1] * w[:, :, 3:4]

    slots = jnp.einsum(
        "zrs,zrd->zsd", dispatch, column[:, :, :width], preferred_element_type=f32
    ).astype(bf16)
    sent = slots.reshape(Z, X, CAP, width)
    items = lax.all_to_all(sent, "x", split_axis=1, concat_axis=1, tiled=True)
    flat = items.reshape(Z * X * CAP, width)
    total = None
    for gate, up, down in zip(gates, ups, downs):
        g = jnp.dot(flat, gate, preferred_element_type=f32)
        u = jnp.dot(flat, up, preferred_element_type=f32)
        hidden = (jax.nn.silu(g) * u).astype(bf16)
        part = jnp.dot(hidden, down, preferred_element_type=f32)
        total = part if total is None else total + part
    back = total.astype(bf16).reshape(Z, X, CAP, width)
    back = lax.all_to_all(back, "x", split_axis=1, concat_axis=1, tiled=True)
    back = back.reshape(Z, half_slots, width)
    moe = jnp.einsum("zrs,zsd->zrd", comb_hi, back, preferred_element_type=f32)
    moe = moe + jnp.einsum("zrs,zsd->zrd", comb_lo, back, preferred_element_type=f32)
    moe = lax.psum_scatter(moe.astype(bf16), "z", scatter_dimension=0, tiled=True)[0]

    kept = jnp.dot(pick, stream, preferred_element_type=f32)
    done = root_norm(kept + moe.astype(f32), final_gain).astype(bf16)
    return jnp.dot(pick.T, done, preferred_element_type=f32).astype(bf16)


def solution(mesh):
    fine = Mesh(mesh.devices.reshape(X, Z, C, -1), ("x", "z", "c", "tp"))
    req = ("x", "z", "c")
    placed = (
        P(req, "tp"),
        P("tp", None),
        P((*req, "tp"), None),
        P(),
        P(),
        P(),
        P(req, None, None),
        P(req, None, None),
        P(req, None, None),
        P((*req, "tp")),
        P((*req, "tp"), None),
    )
    return jax.shard_map(
        shards, mesh=fine, in_specs=placed, out_specs=P((*req, "tp"), None), check_vma=False
    )
```

time: 665 us -> 295 us (0.44)
  waiting for transfers between devices: 398 us -> 194 us
  blocking collectives: 195 us -> 0 us
  matrix products: 31.8 us -> 55.4 us
  local copies, waits for them, and re-layouts: 3.05 us -> 16.9 us
  other arithmetic: 12.9 us -> 2.2 us
    all_to_all x1 -> x2, waiting for transfers between devices: 365 us -> 84.7 us  [the longest x1 43.4 us: shards(): items = lax.all_to_all(sent, 'x', split_axis=1, concat_axis=1, tiled=True)]
    all_to_all x1 -> x0, blocking collectives: 195 us -> none  [shards(): lax.all_to_all(copies, 'req', split_axis=0, concat_axis=0, tiled=True)]
    all_gather x0 -> x1, waiting for transfers between devices: none -> 43.4 us  [shards(): lax.all_gather(jnp.concatenate([picked, meta], axis=1), 'z', axis=0)]
    reduce_scatter x1 -> x2, waiting for transfers between devices: 33 us -> 66.3 us  [the longest x1 40 us: shards(): lax.psum_scatter(moe.astype(bf16), 'z', scatter_dimension=0, tiled=True)[0]]
    dot_general x7 -> x13, matrix products: 31.8 us -> 55.4 us  [the longest x2 27.9 us: shards(): part = jnp.dot(hidden, down, preferred_element_type=f32)]
    reduce_sum x4 -> x1, other arithmetic: 9.51 us -> 0.03 us  [shards(): chosen = jnp.sum(logits[:, None, :] * onehot.astype(f32), axis=-1)]
    reshape x2 -> x4, local copies, waits for them, and re-layouts: 0.21 us -> 7.21 us  [the longest x1 4.71 us: shards(): back = total.astype(bf16).reshape(Z, X, CAP, width)]
  transfers between devices with their start and end apart: 2 -> 8, of which waited for: 2 -> 5; matrix products, arithmetic and copies ran while one was open for 0% -> 11% of each run, Pallas kernels for 0% -> 0%
where the time goes in v1:
time: 295 us; the launch traced here: 294 us
  waiting for transfers between devices  194 us (66%)
  matrix products  55.4 us (19%)
  local copies, waits for them, and re-layouts  16.9 us (6%)
  between operations  13.3 us (5%)
  starting transfers between devices  12.2 us (4%)
    all_to_all x1, waiting for transfers between devices, shards(): items = lax.all_to_all(sent, 'x', split_axis=1, concat_axis=1, tiled=True)  43.4 us
    all_gather x1, waiting for transfers between devices, shards(): lax.all_gather(jnp.concatenate([picked, meta], axis=1), 'z', axis=0)  43.4 us
    all_to_all x1, waiting for transfers between devices, shards(): back = lax.all_to_all(back, 'x', split_axis=1, concat_axis=1, tiled=True)  41.3 us
    reduce_scatter x1, waiting for transfers between devices, shards(): lax.psum_scatter(moe.astype(bf16), 'z', scatter_dimension=0, tiled=True)[0]  40 us
    dot_general x2, matrix products, shards(): part = jnp.dot(hidden, down, preferred_element_type=f32)  27.9 us
    reduce_scatter x1, waiting for transfers between devices, shards(): lax.psum_scatter(jnp.dot(attn_values, out_proj, preferred_element_type=f3...  26.3 us
    dot_general x2, matrix products, shards(): u = jnp.dot(flat, up, preferred_element_type=f32)  14.9 us
    all_to_all x1, starting transfers between devices, shards(): back = lax.all_to_all(back, 'x', split_axis=1, concat_axis=1, tiled=True)  6.26 us
  transfers between devices with their start and end apart: 8, of which 5 were waited for; matrix products, arithmetic and copies ran while one was open for 11% of the time, Pallas kernels for 0%

profile of v1, /device:TPU:10, one launch (start us, length us, event | category | flops | bytes accessed | tf_op | source)
XLA Modules:
  0.0 294.5 jit_solution(16827156330242390159)
XLA Ops:
  6.6 1.5 copy-done
  8.1 2.6 convolution_convert_fusion.1
  11.1 0.2 fusion.15
  11.3 0.2 reshape.42
  11.6 26.3 %reduce-scatter.3.cloned.1.call-done = bf16[64,2048]{1,0:T(8,128)(2,1)} async-done(((bf16[256,2048]{1,0:T(8,128)(2,1)}), bf16[64,2048]{1,0:T(8,128)(2,1)}) %reduce-scatter.3.cloned.1.call-update) | async-done | bytes 262160 | tf_op jit(solution)/shard_map/reduce_scatter | solution.py:40
  37.9 1.1 fusion.23
  39.1 1.2 convolution_convert_fusion.3
  40.3 0.2 fusion.56
  40.7 0.7 fusion.27
  41.5 43.4 %all-gather.3.cloned.1.call-done = bf16[512,2176]{1,0:T(8,128)(2,1)} async-done(((bf16[64,2176]{1,0:T(8,128)(2,1)}), bf16[512,2176]{1,0:T(8,128)(2,1)}) %all-gather.3.cloned.1.call-update) | async-done | bytes 2228240 | tf_op jit(solution)/shard_map/all_gather | solution.py:69
  84.9 0.9 slice.51
  85.9 0.2 fusion.26
  86.1 2.9 convolution_convert_fusion
  89.0 2.3 copy.95
  91.3 5.4 %all-to-all-start = ((bf16[8,4,32,2048]{3,2,0,1:T(8,128)(2,1)}), bf16[8,4,32,2048]{3,2,0,1:T(8,128)(2,1)}, u32[]{:S(2)}, u32[]{:S(2)}) async-start(bf16[8,4,32,2048]{3,2,0,1:T(8,128)(2,1)} %copy.95), calls=%async_computation.1 | async-start | bytes 8388608 | tf_op jit(solution)/shard_map/all_to_all | solution.py:83
  96.7 0.5 collective-permute-start
  97.2 43.4 %all-to-all-done = bf16[8,4,32,2048]{3,2,0,1:T(8,128)(2,1)} async-done(((bf16[8,4,32,2048]{3,2,0,1:T(8,128)(2,1)}), bf16[8,4,32,2048]{3,2,0,1:T(8,128)(2,1)}, u32[]{:S(2)}, u32[]{:S(2)}) %all-to-all-start) | async-done | bytes 4194336 | tf_op jit(solution)/shard_map/all_to_all | solution.py:83
  140.6 2.5 copy.96
  143.1 8.2 %fusion.7 = f32[1024,640]{1,0:T(8,128)} fusion(bf16[1024,2048]{1,0:T(8,128)(2,1)S(1)} %bitcast.69, bf16[1,2048,640]{2,1,0:T(8,128)(2,1)} %param.18), kind=kOutput, calls=%fused_computation.10 | convolution fusion | flops 2684354560 | bytes 9437184 | tf_op jit(solution)/shard_map/dot_general | solution.py:88
  151.4 6.7 %fusion.1 = f32[1024,640]{1,0:T(8,128)} fusion(bf16[1024,2048]{1,0:T(8,128)(2,1)S(1)} %bitcast.70, bf16[1,2048,640]{2,1,0:T(8,128)(2,1)} %collective-permute-done.1), kind=kOutput, calls=%fused_computation.4 | convolution fusion | flops 2684354560 | bytes 9437184 | tf_op jit(solution)/shard_map/dot_general | solution.py:88
  158.0 13.5 %fusion.5 = f32[1024,2048]{1,0:T(8,128)} fusion(bf16[1,640,2048]{2,1,0:T(8,128)(2,1)} %param.19, f32[1024,640]{1,0:T(8,128)} %fusion.7, bf16[1024,2048]{1,0:T(8,128)(2,1)} %bitcast.71, bf16[1,2048,640]{2,1,0:T(8,128)(2,1)} %param.17), kind=kOutput, calls=%fused_computation.8 | convolution fusion | flops 5372641280 | bytes 20447232 | tf_op jit(solution)/shard_map/dot_general | solution.py:90
  171.5 14.4 %add_convert_fusion = bf16[1024,2048]{1,0:T(8,128)(2,1)} fusion(f32[1024,2048]{1,0:T(8,128)} %fusion.5, bf16[1,640,2048]{2,1,0:T(8,128)(2,1)} %collective-permute-done.2, f32[1024,640]{1,0:T(8,128)} %fusion.1, bf16[1024,2048]{1,0:T(8,128)(2,1)} %bitcast.72, bf16[1,2048,640]{2,1,0:T(8,128)(2,1)} %collective-permute-done), kind=kOutput, calls=%fused_computation | convolution fusion | flops 5376835584 | bytes 24641536 | tf_op jit(solution)/shard_map/dot_general | solution.py:90
  185.9 4.7 %copy.97 = bf16[8,4,32,2048]{3,2,0,1:T(8,128)(2,1)} copy(bf16[8,4,32,2048]{3,2,1,0:T(8,128)(2,1)} %bitcast.73) | data formatting | bytes 8388608 | tf_op jit(solution)/shard_map/reshape | solution.py:92
  190.6 6.3 %all-to-all-start.1 = ((bf16[8,4,32,2048]{3,2,0,1:T(8,128)(2,1)}), bf16[8,4,32,2048]{3,2,0,1:T(8,128)(2,1)}, u32[]{:S(2)}, u32[]{:S(2)}) async-start(bf16[8,4,32,2048]{3,2,0,1:T(8,128)(2,1)} %copy.97), calls=%async_computation.2 | async-start | bytes 8388608 | tf_op jit(solution)/shard_map/all_to_all | solution.py:93
  196.9 1.8 slice_reduce_fusion.1
  198.6 41.3 %all-to-all-done.1 = bf16[8,4,32,2048]{3,2,0,1:T(8,128)(2,1)} async-done(((bf16[8,4,32,2048]{3,2,0,1:T(8,128)(2,1)}), bf16[8,4,32,2048]{3,2,0,1:T(8,128)(2,1)}, u32[]{:S(2)}, u32[]{:S(2)}) %all-to-all-start.1) | async-done | bytes 4194336 | tf_op jit(solution)/shard_map/all_to_all | solution.py:93
  239.9 2.5 copy.98
  242.4 0.8 fusion.37
  243.2 2.3 add_convert_fusion.1
  245.6 40.0 %reduce-scatter.5.cloned.1.call-done = bf16[1,64,2048]{2,1,0:T(8,128)(2,1)} async-done(((bf16[8,64,2048]{2,1,0:T(8,128)(2,1)}), bf16[1,64,2048]{2,1,0:T(8,128)(2,1)}) %reduce-scatter.5.cloned.1.call-update) | async-done | bytes 262160 | tf_op jit(solution)/shard_map/reduce_scatter | solution.py:97
  285.5 1.3 multiply_reduce_fusion
  286.9 1.1 convolution_convert_fusion.2
  (47 shorter events, 0.9 us)
Async XLA Ops:
  6.5 1.6 copy-start
  6.5 4.3 %copy-start.7 = (bf16[2048]{0:T(1024)(128)(2,1)S(1)}, bf16[2048]{0:T(1024)(128)(2,1)}, u32[]{:S(2)}) copy-start(bf16[2048]{0:T(1024)(128)(2,1)} %param.14) | copy-start | bytes 12292
  6.5 4.3 %copy-start.6 = (s32[64,2]{0,1:T(2,128)S(1)}, s32[64,2]{0,1:T(2,128)}, u32[]{:S(2)}) copy-start(s32[64,2]{0,1:T(2,128)} %param.21) | copy-start | bytes 1540
  6.5 5.0 %copy-start.9 = (s32[64]{0:T(128)S(1)}, s32[64]{0:T(128)}, u32[]{:S(2)}) copy-start(s32[64]{0:T(128)} %param.20) | copy-start | bytes 772
  6.5 31.4 %copy-start.3 = (bf16[64,2048]{1,0:T(8,128)(2,1)S(1)}, bf16[64,2048]{1,0:T(8,128)(2,1)}, u32[]{:S(2)}) copy-start(bf16[64,2048]{1,0:T(8,128)(2,1)} %param.13) | copy-start | bytes 786436
  6.5 33.8 %copy-start.5 = (bf16[2048,8]{0,1:T(8,128)(2,1)S(1)}, bf16[2048,8]{0,1:T(8,128)(2,1)}, u32[]{:S(2)}) copy-start(bf16[2048,8]{0,1:T(8,128)(2,1)} %param.16) | copy-start | bytes 98308
  6.6 31.4 %reduce-scatter.3.cloned.1.call-start = ((), (), s32[]{:S(2)}) async-start(), calls=%async_computation.4 | async-start | bytes 1310720 | tf_op jit(solution)/shard_map/reduce_scatter | solution.py:40
  10.8 74.1 %all-gather.3.cloned.1.call-start = ((), (), s32[]{:S(2)}) async-start(), calls=%async_computation.6 | async-start | bytes 2506752 | tf_op jit(solution)/shard_map/all_gather | solution.py:69
  91.3 49.3 %all-to-all-start = ((bf16[8,4,32,2048]{3,2,0,1:T(8,128)(2,1)}), bf16[8,4,32,2048]{3,2,0,1:T(8,128)(2,1)}, u32[]{:S(2)}, u32[]{:S(2)}) async-start(bf16[8,4,32,2048]{3,2,0,1:T(8,128)(2,1)} %copy.95), calls=%async_computation.1 | async-start | bytes 8388608 | tf_op jit(solution)/shard_map/all_to_all | solution.py:83
  96.7 54.7 %collective-permute-start.1 = (bf16[1,2048,640]{2,1,0:T(8,128)(2,1)}, bf16[1,2048,640]{2,1,0:T(8,128)(2,1)}, u32[]{:S(2)}, u32[]{:S(2)}) collective-permute-start(bf16[1,2048,640]{2,1,0:T(8,128)(2,1)} %param.18), channel_id=1, source_target_pairs={{0,4},{4,0},{1,5},{5,1},{2,6},{6,2},{3,7},{7,3},{8,12},{12,8},{9,1... | collective-permute-start | bytes 7864328 | tf_op jit(solution)/shard_map/ppermute | solution.py:37
  96.7 74.8 %collective-permute-start = (bf16[1,2048,640]{2,1,0:T(8,128)(2,1)}, bf16[1,2048,640]{2,1,0:T(8,128)(2,1)}, u32[]{:S(2)}, u32[]{:S(2)}) collective-permute-start(bf16[1,2048,640]{2,1,0:T(8,128)(2,1)} %param.17), channel_id=1, source_target_pairs={{0,4},{4,0},{1,5},{5,1},{2,6},{6,2},{3,7},{7,3},{8,12},{12,8},{9,1... | collective-permute-start | bytes 7864328 | tf_op jit(solution)/shard_map/ppermute | solution.py:36
  97.2 74.3 %collective-permute-start.2 = (bf16[1,640,2048]{2,1,0:T(8,128)(2,1)}, bf16[1,640,2048]{2,1,0:T(8,128)(2,1)}, u32[]{:S(2)}, u32[]{:S(2)}) collective-permute-start(bf16[1,640,2048]{2,1,0:T(8,128)(2,1)} %param.19), channel_id=1, source_target_pairs={{0,4},{4,0},{1,5},{5,1},{2,6},{6,2},{3,7},{7,3},{8,12},{12,8},{9,1... | collective-permute-start | bytes 7864328 | tf_op jit(solution)/shard_map/ppermute | solution.py:38
  143.1 8.3 %copy-start.2 = (bf16[8,4,32,2048]{3,2,1,0:T(8,128)(2,1)}, bf16[8,4,32,2048]{3,2,1,0:T(8,128)(2,1)S(1)}, u32[]{:S(2)}) copy-start(bf16[8,4,32,2048]{3,2,1,0:T(8,128)(2,1)S(1)} %copy.96) | copy-start | bytes 12582916
  190.6 49.3 %all-to-all-start.1 = ((bf16[8,4,32,2048]{3,2,0,1:T(8,128)(2,1)}), bf16[8,4,32,2048]{3,2,0,1:T(8,128)(2,1)}, u32[]{:S(2)}, u32[]{:S(2)}) async-start(bf16[8,4,32,2048]{3,2,0,1:T(8,128)(2,1)} %copy.97), calls=%async_computation.2 | async-start | bytes 8388608 | tf_op jit(solution)/shard_map/all_to_all | solution.py:93
  196.9 88.6 %reduce-scatter.5.cloned.1.call-start = ((), (), s32[]{:S(2)}) async-start(), calls=%async_computation.5 | async-start | bytes 2359296 | tf_op jit(solution)/shard_map/reduce_scatter | solution.py:97
  243.2 2.3 copy-start.8
  243.2 42.3 %copy-start.4 = (bf16[64,2048]{1,0:T(8,128)(2,1)S(1)}, bf16[64,2048]{1,0:T(8,128)(2,1)}, u32[]{:S(2)}) copy-start(bf16[64,2048]{1,0:T(8,128)(2,1)} %reduce-scatter.3.cloned.1.call-done) | copy-start | bytes 786436
  243.2 44.7 %copy-start.1 = (bf16[512,2048]{1,0:T(8,128)(2,1)S(1)}, bf16[512,2048]{1,0:T(8,128)(2,1)}, u32[]{:S(2)}) copy-start(bf16[512,2048]{1,0:T(8,128)(2,1)} %param.12) | copy-start | bytes 6291460
Sparse Core Ops, SparseCore 0:
  10.9 26.9 reduce-scatter.2
  41.6 43.2 all-gather.2
  245.7 39.8 reduce-scatter.4

commit v2 on v1

v2 whole, which is shorter than its diff:
```python
import functools

import jax
import jax.numpy as jnp
from jax import lax
from jax.experimental import pallas as pl
from jax.experimental.pallas import tpu as pltpu
from jax.sharding import Mesh, PartitionSpec as P

TOP = 2
CAP = 32
X, Z, C = 4, 8, 2
HALF = X * CAP
META = 128
MESH = pl.DeviceIdType.MESH
F32, BF16 = jnp.float32, jnp.bfloat16


def root_norm(values, gain):
    mean_sq = jnp.mean(values * values, axis=-1, keepdims=True)
    return values * lax.rsqrt(mean_sq + 1e-06) * gain.astype(F32)


def greet(peers):
    barrier = pltpu.get_barrier_semaphore()
    for peer in peers:
        pl.semaphore_signal(barrier, inc=1, device_id=peer, device_id_type=MESH)
    return lambda: pl.semaphore_wait(barrier, len(peers))


def remote(src, dst, send, recv, peer):
    copy = pltpu.make_async_remote_copy(
        src_ref=src, dst_ref=dst, send_sem=send, recv_sem=recv,
        device_id=peer, device_id_type=MESH,
    )
    copy.start()
    return copy


def x_peer(mx, d):
    return {"x": lax.rem(mx + d, X)}


def front(
    tp, attn, proj, resid, gain, router, pick, first, second, places, gate, up, down,
    items, meta, kept, gate2, up2, down2,
    part, inbox, chunk, col, slots,
    tp_send, tp_recv, z_send, z_recv, x_send, x_recv, own_sem, w_send, w_recv,
):
    mx, mz = lax.axis_index("x"), lax.axis_index("z")
    mc, mt = lax.axis_index("c"), lax.axis_index("tp")
    rows, width = resid.shape
    above, below = {"z": lax.rem(mz + 1, Z)}, {"z": lax.rem(mz + Z - 1, Z)}
    other = {"c": 1 - mc}
    mates = [{"tp": lax.rem(mt + d, tp)} for d in range(1, tp)]
    ready = greet(mates + [above, below, other] + [x_peer(mx, d) for d in range(1, X)])

    def term(t):
        block = attn[pl.ds(pl.multiple_of(t * rows, rows), rows), :]
        return jnp.dot(block, proj[...], preferred_element_type=F32)

    pending = []
    for d in range(1, tp):
        part[d - 1] = term(lax.rem(mt + d, tp)).astype(BF16)
        if d == 1:
            ready()
        pending.append(
            remote(part.at[d - 1], inbox.at[d - 1], tp_send.at[d - 1], tp_recv.at[d - 1], mates[d - 1])
        )
    swaps = [
        remote(a, b, w_send.at[i], w_recv.at[i], other)
        for i, (a, b) in enumerate(((gate, gate2), (up, up2), (down, down2)))
    ]
    total = term(mt)
    for d in range(1, tp):
        pending[d - 1].wait_recv()
        total = total + inbox[d - 1].astype(F32)
    stream = (resid[...].astype(F32) + total).astype(BF16)
    normed = root_norm(stream.astype(F32), gain[...]).astype(BF16)
    picked = jnp.dot(pick[...], normed, preferred_element_type=F32).astype(BF16)
    kept[...] = jnp.dot(pick[...], stream, preferred_element_type=F32).astype(BF16)
    logits = jnp.dot(picked, router[...], preferred_element_type=F32)
    chosen_a = jnp.sum(logits * first[...], axis=-1, keepdims=True)
    chosen_b = jnp.sum(logits * second[...], axis=-1, keepdims=True)
    lane = lax.broadcasted_iota(jnp.int32, (rows, META), 1)
    notes = places[...]
    for i, w in enumerate((jax.nn.sigmoid(chosen_a - chosen_b), jax.nn.sigmoid(chosen_b - chosen_a))):
        high = w.astype(BF16).astype(F32)
        notes = notes + jnp.where(lane == 2 + i, high, 0.0)
        notes = notes + jnp.where(lane == 4 + i, w - high, 0.0)
    chunk[:, :width] = picked
    chunk[:, width:] = notes.astype(BF16)

    offset = (mz // (Z // 2) * HALF).astype(F32)
    at = lane.astype(F32)
    exchanged = []

    def spread(order, zs, block):
        note = block[:, width:]
        meta[zs] = note
        wide = note.astype(F32)
        hit = (wide[:, 0:1] - offset == at) | (wide[:, 1:2] - offset == at)
        table = jnp.where(hit, 1.0, 0.0).astype(BF16)
        found = lax.dot_general(
            table, block[:, :width], (((0,), (0,)), ((), ())), preferred_element_type=F32
        )
        slots[zs] = found.astype(BF16).reshape(X, CAP, width)
        for d in range(1, X):
            peer = x_peer(mx, d)
            exchanged.append(
                remote(
                    slots.at[zs, peer["x"]], items.at[zs, mx],
                    x_send.at[order, d - 1], x_recv.at[order, d - 1], peer,
                )
            )
        own = pltpu.make_async_copy(slots.at[zs, mx], items.at[zs, mx], own_sem.at[order])
        own.start()
        exchanged.append(own)

    far = Z // 2
    upper, lower = slice(0, rows // 2), slice(rows // 2, rows)
    rising = [remote(chunk, col.at[mz], z_send.at[0, 0], z_recv.at[0, 0], above)]
    falling = [remote(chunk, col.at[mz], z_send.at[1, 0], z_recv.at[1, 0], below)]
    spread(0, mz, chunk)
    for k in range(1, far):
        low, high = lax.rem(mz + Z - k, Z), lax.rem(mz + k, Z)
        a, b = col.at[low], col.at[high]
        if k == far - 1:
            a, b = col.at[low, upper], col.at[high, lower]
        rising[k - 1].wait_recv()
        rising.append(remote(a, a, z_send.at[0, k], z_recv.at[0, k], above))
        falling[k - 1].wait_recv()
        falling.append(remote(b, b, z_send.at[1, k], z_recv.at[1, k], below))
        spread(2 * k - 1, low, col.at[low])
        spread(2 * k, high, col.at[high])
    last = lax.rem(mz + far, Z)
    rising[-1].wait_recv()
    falling[-1].wait_recv()
    spread(Z - 1, last, col.at[last])
    for copy in pending + rising + falling:
        copy.wait_send()
    for copy in exchanged + swaps:
        copy.wait()


def back(
    partial, meta, kept, pick, gain, out,
    got, part, inbox, x_send, x_recv, own_sem, z_send, z_recv,
):
    mx, mz = lax.axis_index("x"), lax.axis_index("z")
    rows, width = kept.shape
    greet(
        [{"z": lax.rem(mz + d, Z)} for d in range(1, Z)] + [x_peer(mx, d) for d in range(1, X)]
    )()
    far = Z // 2
    steps = [far]
    for k in range(far - 1, 0, -1):
        steps += [k, Z - k]
    steps.append(0)
    coming, going = [], []
    for o, s in enumerate(steps):
        zs = lax.rem(mz + s, Z)
        copies = []
        for d in range(1, X):
            peer = x_peer(mx, d)
            copies.append(
                remote(
                    partial.at[zs, peer["x"]], got.at[zs, mx],
                    x_send.at[o, d - 1], x_recv.at[o, d - 1], peer,
                )
            )
        own = pltpu.make_async_copy(partial.at[zs, mx], got.at[zs, mx], own_sem.at[o])
        own.start()
        coming.append((copies, own))
    offset = (mz // (Z // 2) * HALF).astype(F32)
    at = lax.broadcasted_iota(jnp.int32, (rows, HALF), 1).astype(F32)
    total = None
    for o, s in enumerate(steps):
        zs = lax.rem(mz + s, Z)
        note = meta[zs].astype(F32)
        hit_a, hit_b = note[:, 0:1] - offset == at, note[:, 1:2] - offset == at
        high = jnp.where(hit_a, note[:, 2:3], 0.0) + jnp.where(hit_b, note[:, 3:4], 0.0)
        low = jnp.where(hit_a, note[:, 4:5], 0.0) + jnp.where(hit_b, note[:, 5:6], 0.0)
        copies, own = coming[o]
        own.wait()
        for copy in copies:
            copy.wait_recv()
        block = got[zs].reshape(HALF, width)
        value = jnp.dot(high.astype(BF16), block, preferred_element_type=F32)
        value = value + jnp.dot(low.astype(BF16), block, preferred_element_type=F32)
        if s == 0:
            total = value
        else:
            part[o] = value.astype(BF16)
            going.append(
                remote(part.at[o], inbox.at[o], z_send.at[o], z_recv.at[o], {"z": zs})
            )
    for o, copy in enumerate(going):
        copy.wait_recv()
        total = total + inbox[o].astype(F32)
    done = root_norm(kept[...].astype(F32) + total, gain[...]).astype(BF16)
    out[...] = lax.dot_general(
        pick[...], done, (((0,), (0,)), ((), ())), preferred_element_type=F32
    ).astype(BF16)
    for copies, _ in coming:
        for copy in copies:
            copy.wait_send()
    for copy in going:
        copy.wait_send()


def shards(
    attn_values,
    out_proj,
    residual_in,
    norm_gain,
    final_gain,
    router,
    gate_weight,
    up_weight,
    down_weight,
    row_order,
    routes,
):
    rows, width = residual_in.shape
    experts = router.shape[1]
    tp = lax.axis_size("tp")
    shape = jax.ShapeDtypeStruct
    dma = pltpu.SemaphoreType.DMA
    vmem = pl.BlockSpec(memory_space=pltpu.VMEM)
    hbm = pl.BlockSpec(memory_space=pl.ANY)

    local_order = lax.rem(row_order, rows)
    pick = (local_order[:, None] == jnp.arange(rows, dtype=jnp.int32)[None, :]).astype(BF16)
    onehot = (routes[:, :, None] == jnp.arange(experts, dtype=jnp.int32)).astype(F32)
    flat_hot = onehot.reshape(rows * TOP, experts)
    earlier = jnp.tri(rows * TOP, k=-1, dtype=BF16)
    before = jnp.dot(earlier, flat_hot.astype(BF16), preferred_element_type=F32)
    rank = jnp.sum(before * flat_hot, axis=-1).reshape(rows, TOP)
    slot = (routes % 2 * HALF + routes // 2 * CAP).astype(F32) + rank
    places = jnp.pad(slot, ((0, 0), (0, META - TOP)))
    wide = ((0, 0), (0, META - experts))
    first, second = jnp.pad(onehot[:, 0], wide), jnp.pad(onehot[:, 1], wide)

    items, meta, kept, gate2, up2, down2 = pl.pallas_call(
        functools.partial(front, tp),
        out_shape=(
            shape((Z, X, CAP, width), BF16),
            shape((Z, rows, META), BF16),
            shape((rows, width), BF16),
            shape(gate_weight.shape[1:], BF16),
            shape(up_weight.shape[1:], BF16),
            shape(down_weight.shape[1:], BF16),
        ),
        in_specs=[vmem] * 9 + [hbm] * 3,
        out_specs=(vmem, vmem, vmem, hbm, hbm, hbm),
        scratch_shapes=[
            pltpu.VMEM((tp - 1, rows, width), BF16),
            pltpu.VMEM((tp - 1, rows, width), BF16),
            pltpu.VMEM((rows, width + META), BF16),
            pltpu.VMEM((Z, rows, width + META), BF16),
            pltpu.VMEM((Z, X, CAP, width), BF16),
            dma((tp - 1,)), dma((tp - 1,)),
            dma((2, Z // 2)), dma((2, Z // 2)),
            dma((Z, X - 1)), dma((Z, X - 1)),
            dma((Z,)), dma((3,)), dma((3,)),
        ],
        compiler_params=pltpu.CompilerParams(
            collective_id=0, has_side_effects=True, vmem_limit_bytes=40 << 20
        ),
        name="front",
    )(
        attn_values, out_proj, residual_in, norm_gain[None], jnp.pad(router, wide), pick,
        first, second, places, gate_weight[0], up_weight[0], down_weight[0],
    )

    flat = items.reshape(Z * X * CAP, width)
    total = None
    for gate, up, down in (
        (gate_weight[0], up_weight[0], down_weight[0]), (gate2, up2, down2)
    ):
        g = jnp.dot(flat, gate, preferred_element_type=F32)
        u = jnp.dot(flat, up, preferred_element_type=F32)
        hidden = (jax.nn.silu(g) * u).astype(BF16)
        value = jnp.dot(hidden, down, preferred_element_type=F32)
        total = value if total is None else total + value

    return pl.pallas_call(
        back,
        out_shape=shape((rows, width), BF16),
        in_specs=[vmem] * 5,
        out_specs=vmem,
        scratch_shapes=[
            pltpu.VMEM((Z, X, CAP, width), BF16),
            pltpu.VMEM((Z - 1, rows, width), BF16),
            pltpu.VMEM((Z - 1, rows, width), BF16),
            dma((Z, X - 1)), dma((Z, X - 1)), dma((Z,)),
            dma((Z - 1,)), dma((Z - 1,)),
        ],
        compiler_params=pltpu.CompilerParams(
            collective_id=1, has_side_effects=True, vmem_limit_bytes=40 << 20
        ),
        name="back",
    )(total.astype(BF16).reshape(Z, X, CAP, width), meta, kept, pick, final_gain[None])


def solution(mesh):
    fine = Mesh(mesh.devices.reshape(X, Z, C, -1), ("x", "z", "c", "tp"))
    req = ("x", "z", "c")
    placed = (
        P(req, "tp"),
        P("tp", None),
        P((*req, "tp"), None),
        P(),
        P(),
        P(),
        P(req, None, None),
        P(req, None, None),
        P(req, None, None),
        P((*req, "tp")),
        P((*req, "tp"), None),
    )
    return jax.shard_map(
        shards, mesh=fine, in_specs=placed, out_specs=P((*req, "tp"), None), check_vma=False
    )
```

time: 295 us -> 193 us (0.65); the launches traced: 294 us -> 189 us
  waiting for transfers between devices: 194 us -> 0 us
  Pallas kernels: 0 us -> 130 us
  between operations: 13.3 us -> 0.13 us
  matrix products: 55.4 us -> 43 us
  starting transfers between devices: 12.2 us -> 0 us
    pallas_call x0 -> x2, Pallas kernels: none -> 130 us  [the longest x1 72.7 us: shards(): pl.pallas_call(functools.partial(front, tp), out_shape=(shape((Z, X, CAP,...]
    all_to_all x2 -> x0, waiting for transfers between devices: 84.7 us -> none  [the longest x1 43.4 us: shards(): items = lax.all_to_all(sent, 'x', split_axis=1, concat_axis=1, tiled=True)]
    reduce_scatter x2 -> x0, waiting for transfers between devices: 66.3 us -> none  [the longest x1 40 us: shards(): lax.psum_scatter(moe.astype(bf16), 'z', scatter_dimension=0, tiled=True)[0]]
    all_gather x1 -> x0, waiting for transfers between devices: 43.4 us -> none  [shards(): lax.all_gather(jnp.concatenate([picked, meta], axis=1), 'z', axis=0)]
    dot_general x13 -> x5, matrix products: 55.4 us -> 43 us  [the longest x2 27.8 us: shards(): value = jnp.dot(hidden, down, preferred_element_type=F32)]
    all_to_all x2 -> x0, starting transfers between devices: 11.6 us -> none  [the longest x1 6.26 us: shards(): back = lax.all_to_all(back, 'x', split_axis=1, concat_axis=1, tiled=True)]
    unnamed x23 -> x21, local copies, waits for them, and re-layouts: 1.9 us -> 13 us
    reshape x4 -> x1, local copies, waits for them, and re-layouts: 7.21 us -> 0.15 us  [shards(): rank = jnp.sum(before * flat_hot, axis=-1).reshape(rows, TOP)]
  transfers between devices with their start and end apart: 8 -> 0, of which waited for: 5 -> 0; matrix products, arithmetic and copies ran while one was open for 11% -> 0% of each run, Pallas kernels for 0% -> 0%
where the time goes in v2:
time: 193 us; the launch traced here: 189 us
  Pallas kernels  130 us (67%)
  matrix products  43 us (22%)
  local copies, waits for them, and re-layouts  14.2 us (7%)
  other arithmetic  2.24 us (1%)
    pallas_call x1, Pallas kernels, shards(): pl.pallas_call(functools.partial(front, tp), out_shape=(shape((Z, X, CAP,...  72.7 us
    pallas_call x1, Pallas kernels, shards(): pl.pallas_call(back, out_shape=shape((rows, width), BF16), in_specs=[vmem...  57.1 us
    dot_general x2, matrix products, shards(): value = jnp.dot(hidden, down, preferred_element_type=F32)  27.8 us
    dot_general x2, matrix products, shards(): g = jnp.dot(flat, gate, preferred_element_type=F32)  15 us
    unnamed x21, local copies, waits for them, and re-layouts  13 us

profile of v2, /device:TPU:10, one launch (start us, length us, event | category | flops | bytes accessed | tf_op | source)
XLA Modules:
  0.0 189.4 jit_solution(17278221759361707973)
XLA Ops:
  0.0 0.0 copy-start.2
  0.0 0.9 copy.23
  0.9 0.1 eq.43
  1.1 0.2 fusion
  1.3 0.2 reshape.13
  1.4 0.7 broadcast_compare_fusion
  2.1 0.1 copy.26
  2.3 0.8 fusion.2
  3.1 0.7 compare_select_fusion
  3.8 0.1 fusion.11.pick
  3.9 1.0 copy.21
  4.9 0.1 pad.15.router
  5.0 0.7 broadcast_in_dim.4.gain
  5.7 0.0 copy-done.2
  5.7 0.0 copy-start.1
  5.7 1.7 copy-done.1
  7.5 0.9 copy-done.3
  8.4 0.9 copy-done.4
  9.4 72.7 %front.1 = (bf16[8,4,32,2048]{3,2,1,0:T(8,128)(2,1)}, bf16[8,64,128]{2,1,0:T(8,128)(2,1)S(1)}, bf16[64,2048]{1,0:T(8,128)(2,1)S(1)}, bf16[2048,640]{1,0:T(8,128)...) custom-call(bf16[256,512]{1,0:T(8,128)(2,1)S(1)} %copy-done.3, bf16[512,2048]{1,0:T(8,128)(2,1)S(1)} %copy-done.2, ...), custom_call_target="tpu_custom_call" | custom-call | tf_op jit(solution)/shard_map/front/pallas_call | solution.py:245
  82.1 0.0 copy-start.5
  82.1 1.5 copy-done.5
  83.6 1.5 copy-done.6
  85.1 1.5 copy-done.7
  86.6 7.1 %fusion.19 = f32[1024,640]{1,0:T(8,128)} fusion(bf16[1024,2048]{1,0:T(8,128)(2,1)} %bitcast.27, bf16[1,2048,640]{2,1,0:T(8,128)(2,1)S(1)} %copy-done.1), kind=kOutput, calls=%fused_computation.39 | convolution fusion | flops 2684354560 | bytes 9437184 | tf_op jit(solution)/shard_map/dot_general | solution.py:282
  93.7 13.4 %fusion.1 = f32[1024,2048]{1,0:T(8,128)} fusion(f32[1024,640]{1,0:T(8,128)} %fusion.19, bf16[1024,2048]{1,0:T(8,128)(2,1)} %bitcast.28, bf16[1,640,2048]{2,1,0:T(8,128)(2,1)} %param.19, bf16[1,2048,640]{2,1,0:T(8,128)(2,1)} %param.18), kind=kOutput, calls=%fused_computation.5 | convolution fusion | flops 5372641280 | bytes 20447232 | tf_op jit(solution)/shard_map/dot_general | solution.py:285
  107.1 7.9 %fusion.23 = f32[1024,640]{1,0:T(8,128)} fusion(bf16[1024,2048]{1,0:T(8,128)(2,1)} %bitcast.29, bf16[2048,640]{1,0:T(8,128)(2,1)} %copy-done.7), kind=kOutput, calls=%fused_computation.43 | convolution fusion | flops 2684354560 | bytes 9437184 | tf_op jit(solution)/shard_map/dot_general | solution.py:282
  115.0 14.3 %add_convert_fusion = bf16[1024,2048]{1,0:T(8,128)(2,1)} fusion(f32[1024,2048]{1,0:T(8,128)} %fusion.1, bf16[640,2048]{1,0:T(8,128)(2,1)} %copy-done.6, f32[1024,640]{1,0:T(8,128)} %fusion.23, bf16[1024,2048]{1,0:T(8,128)(2,1)} %bitcast.30, bf16[2048,640]{1,0:T(8,128)(2,1)} %copy-done.5), kind=kOutput, calls=%fused_computation | convolution fusion | flops 5376835584 | bytes 24641536 | tf_op jit(solution)/shard_map/dot_general | solution.py:285
  129.4 0.0 copy-done.8
  129.4 0.0 copy-start
  129.4 2.2 %copy-done = bf16[1024,2048]{1,0:T(8,128)(2,1)S(1)} copy-done((bf16[1024,2048]{1,0:T(8,128)(2,1)S(1)}, bf16[1024,2048]{1,0:T(8,128)(2,1)}, u32[]{:S(2)}) %copy-start) | copy-done | bytes 4194328
  131.6 57.1 %back.1 = bf16[64,2048]{1,0:T(8,128)(2,1)S(1)} custom-call(bf16[8,4,32,2048]{3,2,1,0:T(8,128)(2,1)S(1)} %bitcast.23, bf16[8,64,128]{2,1,0:T(8,128)(2,1)S(1)} %get-tuple-element.15.meta, bf16[64,2048]{1,0:T(8,128)(2,1)S(1)} %get-tuple-element.16.kept, bf16[64,64]{1,0:T(8,128)(2,1)S(1)} %fusion.11.pick, bf16[1,2048]{1,0:T(2,128)(2,1)S(1)} %broadcast_in_dim.5.gain), custom_call_target="tpu_custom_call" | custom-call | tf_op jit(solution)/shard_map/back/pallas_call | solution.py:288
  188.7 0.7 copy.31
  (12 shorter events, 0.1 us)
Async XLA Ops:
  0.0 5.7 %copy-start.2 = (bf16[512,2048]{1,0:T(8,128)(2,1)S(1)}, bf16[512,2048]{1,0:T(8,128)(2,1)}, u32[]{:S(2)}) copy-start(bf16[512,2048]{1,0:T(8,128)(2,1)} %proj.1) | copy-start | bytes 6291460
  5.7 1.7 copy-start.1
  7.5 0.9 copy-start.3
  8.4 0.9 copy-start.4
  82.1 1.5 copy-start.5
  83.6 1.5 copy-start.6
  85.1 1.5 copy-start.7
  115.0 14.4 %copy-start.8 = (bf16[2048]{0:T(1024)(128)(2,1)S(1)}, bf16[2048]{0:T(1024)(128)(2,1)}, u32[]{:S(2)}) copy-start(bf16[2048]{0:T(1024)(128)(2,1)} %param.15) | copy-start | bytes 12292
  129.4 2.2 %copy-start = (bf16[1024,2048]{1,0:T(8,128)(2,1)S(1)}, bf16[1024,2048]{1,0:T(8,128)(2,1)}, u32[]{:S(2)}) copy-start(bf16[1024,2048]{1,0:T(8,128)(2,1)} %add_convert_fusion) | copy-start | bytes 12582916

commit v3 on v2

v3 whole, which is shorter than its diff:
```python
import functools

import jax
import jax.numpy as jnp
from jax import lax
from jax.experimental import pallas as pl
from jax.experimental.pallas import tpu as pltpu
from jax.sharding import Mesh, PartitionSpec as P

TOP = 2
CAP = 32
X, Z, C = 4, 8, 2
HALF = X * CAP
META = 128
MESH = pl.DeviceIdType.MESH
F32, BF16 = jnp.float32, jnp.bfloat16


def root_norm(values, gain):
    mean_sq = jnp.mean(values * values, axis=-1, keepdims=True)
    return values * lax.rsqrt(mean_sq + 1e-06) * gain.astype(F32)


def greet(peers):
    barrier = pltpu.get_barrier_semaphore()
    for peer in peers:
        pl.semaphore_signal(barrier, inc=1, device_id=peer, device_id_type=MESH)
    return lambda: pl.semaphore_wait(barrier, len(peers))


def remote(src, dst, send, recv, peer):
    copy = pltpu.make_async_remote_copy(
        src_ref=src, dst_ref=dst, send_sem=send, recv_sem=recv,
        device_id=peer, device_id_type=MESH,
    )
    copy.start()
    return copy


def x_peer(mx, d):
    return {"x": lax.rem(mx + d, X)}


PLACES = (0, -1, -3, 3, 4, -2, 1, 2)


def layer(
    tp, attn, proj, resid, gain, last_gain, router, order, routes, gate, up, down,
    out,
    part, inbox, chunk, col, slots, items, partial, got, tail, tails, hidden,
    gates, ups, downs,
    tp_send, tp_recv, z_send, z_recv, x_send, x_recv, own_sem,
    r_send, r_recv, r_own, t_send, t_recv, w_own, w_send, w_recv,
):
    mx, mz = lax.axis_index("x"), lax.axis_index("z")
    mc, mt = lax.axis_index("c"), lax.axis_index("tp")
    rows, width = resid.shape
    units = gate.shape[1]
    above, below = {"z": lax.rem(mz + 1, Z)}, {"z": lax.rem(mz + Z - 1, Z)}
    other = {"c": 1 - mc}
    mates = [{"tp": lax.rem(mt + d, tp)} for d in range(1, tp)]
    column = [{"z": lax.rem(mz + d, Z)} for d in range(1, Z)]
    ready = greet(mates + column + [other] + [x_peer(mx, d) for d in range(1, X)])

    loads = []
    near, far_side = pl.ds(0, units), pl.ds(units, units)
    for i, (a, b) in enumerate(
        ((gate, gates.at[:, near]), (up, ups.at[:, near]), (down, downs.at[near, :]))
    ):
        copy = pltpu.make_async_copy(a, b, w_own.at[i])
        copy.start()
        loads.append(copy)

    def term(t):
        block = attn[pl.ds(pl.multiple_of(t * rows, rows), rows), :]
        return jnp.dot(block, proj[...], preferred_element_type=F32)

    pending = []
    for d in range(1, tp):
        part[d - 1] = term(lax.rem(mt + d, tp)).astype(BF16)
        if d == 1:
            ready()
        pending.append(
            remote(part.at[d - 1], inbox.at[d - 1], tp_send.at[d - 1], tp_recv.at[d - 1], mates[d - 1])
        )
    swaps = [
        remote(a, b, w_send.at[i], w_recv.at[i], other)
        for i, (a, b) in enumerate(
            ((gate, gates.at[:, far_side]), (up, ups.at[:, far_side]), (down, downs.at[far_side, :]))
        )
    ]
    total = term(mt)

    down_rows = lax.broadcasted_iota(jnp.int32, (rows, rows), 0)
    along = lax.broadcasted_iota(jnp.int32, (rows, rows), 1)
    upright = lambda v: jnp.sum(
        jnp.where(down_rows == along, v.astype(F32), 0.0), axis=1, keepdims=True
    )
    pick_t = jnp.where((order[...] & (rows - 1)) == down_rows, 1.0, 0.0).astype(BF16)
    earlier = jnp.where(along < down_rows, 1.0, 0.0).astype(BF16)
    route = routes[...]
    names = lax.broadcasted_iota(jnp.int32, (rows, router.shape[0]), 1).astype(F32)
    hot = [jnp.where(upright(route[k : k + 1, :]) == names, 1.0, 0.0) for k in range(TOP)]
    before = jnp.dot(earlier, (hot[0] + hot[1]).astype(BF16), preferred_element_type=F32)
    base = (route & 1) * HALF + (route >> 1) * CAP
    lane = lax.broadcasted_iota(jnp.int32, (rows, META), 1)
    notes = jnp.zeros((rows, META), F32)
    for k in range(TOP):
        rank = jnp.sum(before * hot[k], axis=1, keepdims=True)
        notes = notes + jnp.where(lane == k, upright(base[k : k + 1, :]) + rank, 0.0)

    for d in range(1, tp):
        pending[d - 1].wait_recv()
        total = total + inbox[d - 1].astype(F32)
    stream = (resid[...].astype(F32) + total).astype(BF16)
    normed = root_norm(stream.astype(F32), gain[...]).astype(BF16)
    across = (((0,), (0,)), ((), ()))
    picked = lax.dot_general(pick_t, normed, across, preferred_element_type=F32).astype(BF16)
    logits = lax.dot_general(
        picked, router[...], (((1,), (1,)), ((), ())), preferred_element_type=F32
    )
    chosen = [jnp.sum(logits * hot[k], axis=1, keepdims=True) for k in range(TOP)]
    for k in range(TOP):
        w = jax.nn.sigmoid(chosen[k] - chosen[1 - k])
        high = w.astype(BF16).astype(F32)
        notes = notes + jnp.where(lane == 2 + k, high, 0.0)
        notes = notes + jnp.where(lane == 4 + k, w - high, 0.0)
    chunk[:, :width] = picked
    chunk[:, width:] = notes.astype(BF16)

    offset = (mz // (Z // 2) * HALF).astype(F32)
    at = lane.astype(F32)
    sent = {}

    def block_of(p):
        s = PLACES[p]
        return chunk if s == 0 else col.at[lax.rem(mz + s + Z, Z)]

    def spread(p):
        block = block_of(p)
        wide = block[:, width:].astype(F32)
        hit = (wide[:, 0:1] - offset == at) | (wide[:, 1:2] - offset == at)
        table = jnp.where(hit, 1.0, 0.0).astype(BF16)
        found = lax.dot_general(table, block[:, :width], across, preferred_element_type=F32)
        slots[p] = found.astype(BF16).reshape(X, CAP, width)
        copies = []
        for d in range(1, X):
            peer = x_peer(mx, d)
            copies.append(
                remote(
                    slots.at[p, peer["x"]], items.at[p, mx],
                    x_send.at[p, d - 1], x_recv.at[p, d - 1], peer,
                )
            )
        own = pltpu.make_async_copy(slots.at[p, mx], items.at[p, mx], own_sem.at[p])
        own.start()
        sent[p] = copies, own

    far = Z // 2
    upper, lower = slice(0, rows // 2), slice(rows // 2, rows)
    rising = [remote(chunk, col.at[mz], z_send.at[0, 0], z_recv.at[0, 0], above)]
    falling = [remote(chunk, col.at[mz], z_send.at[1, 0], z_recv.at[1, 0], below)]
    spread(0)
    soon = {1: (1, 6), 2: (5,), 3: (2, 3)}
    for k in range(1, far):
        low, high = lax.rem(mz + Z - k, Z), lax.rem(mz + k, Z)
        a, b = col.at[low], col.at[high]
        if k == far - 1:
            a, b = col.at[low, upper], col.at[high, lower]
        rising[k - 1].wait_recv()
        rising.append(remote(a, a, z_send.at[0, k], z_recv.at[0, k], above))
        falling[k - 1].wait_recv()
        falling.append(remote(b, b, z_send.at[1, k], z_recv.at[1, k], below))
        for p in soon[k]:
            spread(p)
    rising[-1].wait_recv()
    falling[-1].wait_recv()
    spread(4)
    spread(7)

    for copy in loads:
        copy.wait()
    for copy in swaps:
        copy.wait_recv()

    tile = 256

    def experts(first):
        for p in (first, first + 1):
            copies, own = sent[p]
            own.wait()
            for copy in copies:
                copy.wait_recv()

        @pl.loop(0, 2 * units // tile)
        def _(j):
            at_j = pl.ds(pl.multiple_of(j * tile, tile), tile)
            flat = items[first : first + 2].reshape(2 * HALF, width)
            g = jnp.dot(flat, gates[:, at_j], preferred_element_type=F32)
            u = jnp.dot(flat, ups[:, at_j], preferred_element_type=F32)
            hidden[:, at_j] = (g / (1.0 + jnp.exp(-g)) * u).astype(BF16)

        @pl.loop(0, width // tile)
        def _(j):
            at_j = pl.ds(pl.multiple_of(j * tile, tile), tile)
            value = jnp.dot(hidden[...], downs[:, at_j], preferred_element_type=F32)
            partial[first : first + 2, :, :, at_j] = value.astype(BF16).reshape(2, X, CAP, tile)

    returned = {}

    def give_back(p):
        copies = []
        for d in range(1, X):
            peer = x_peer(mx, d)
            copies.append(
                remote(
                    partial.at[p, peer["x"]], got.at[p, mx],
                    r_send.at[p, d - 1], r_recv.at[p, d - 1], peer,
                )
            )
        own = pltpu.make_async_copy(partial.at[p, mx], got.at[p, mx], r_own.at[p])
        own.start()
        returned[p] = copies, own

    going = []

    def combine(p):
        note = block_of(p)[:, width:].astype(F32)
        hit_a, hit_b = note[:, 0:1] - offset == at, note[:, 1:2] - offset == at
        high = jnp.where(hit_a, note[:, 2:3], 0.0) + jnp.where(hit_b, note[:, 3:4], 0.0)
        low = jnp.where(hit_a, note[:, 4:5], 0.0) + jnp.where(hit_b, note[:, 5:6], 0.0)
        copies, own = returned[p]
        own.wait()
        for copy in copies:
            copy.wait_recv()
        block = got[p].reshape(HALF, width)
        value = jnp.dot(high.astype(BF16), block, preferred_element_type=F32)
        value = value + jnp.dot(low.astype(BF16), block, preferred_element_type=F32)
        if p == 0:
            return value
        tail[p - 1] = value.astype(BF16)
        peer = {"z": lax.rem(mz + PLACES[p] + Z, Z)}
        going.append(
            remote(tail.at[p - 1], tails.at[p - 1], t_send.at[p - 1], t_recv.at[p - 1], peer)
        )

    experts(0)
    experts(2)
    give_back(2)
    give_back(3)
    experts(4)
    give_back(4)
    give_back(5)
    combine(2)
    combine(3)
    experts(6)
    for p in (7, 6, 1, 0):
        give_back(p)
    for p in (4, 5, 7, 6, 1):
        combine(p)
    total = combine(0)
    for i, copy in enumerate(going):
        copy.wait_recv()
    for i in range(Z - 1):
        total = total + tails[i].astype(F32)
    kept = lax.dot_general(pick_t, stream, across, preferred_element_type=F32)
    done = root_norm(kept + total, last_gain[...]).astype(BF16)
    out[...] = jnp.dot(pick_t, done, preferred_element_type=F32).astype(BF16)
    for copy in pending + rising + falling + swaps + going:
        copy.wait_send()
    for group in (sent, returned):
        for copies, _ in group.values():
            for copy in copies:
                copy.wait_send()


def shards(
    attn_values,
    out_proj,
    residual_in,
    norm_gain,
    final_gain,
    router,
    gate_weight,
    up_weight,
    down_weight,
    row_order,
    routes,
):
    rows, width = residual_in.shape
    units = gate_weight.shape[-1]
    tp = lax.axis_size("tp")
    dma = pltpu.SemaphoreType.DMA
    vmem = pl.BlockSpec(memory_space=pltpu.VMEM)
    hbm = pl.BlockSpec(memory_space=pl.ANY)
    block = pltpu.VMEM((Z, X, CAP, width), BF16)
    return pl.pallas_call(
        functools.partial(layer, tp),
        out_shape=jax.ShapeDtypeStruct((rows, width), BF16),
        in_specs=[vmem] * 8 + [hbm] * 3,
        out_specs=vmem,
        scratch_shapes=[
            pltpu.VMEM((tp - 1, rows, width), BF16),
            pltpu.VMEM((tp - 1, rows, width), BF16),
            pltpu.VMEM((rows, width + META), BF16),
            pltpu.VMEM((Z, rows, width + META), BF16),
            block, block, block, block,
            pltpu.VMEM((Z - 1, rows, width), BF16),
            pltpu.VMEM((Z - 1, rows, width), BF16),
            pltpu.VMEM((2 * HALF, 2 * units), BF16),
            pltpu.VMEM((width, 2 * units), BF16),
            pltpu.VMEM((width, 2 * units), BF16),
            pltpu.VMEM((2 * units, width), BF16),
            dma((tp - 1,)), dma((tp - 1,)),
            dma((2, Z // 2)), dma((2, Z // 2)),
            dma((Z, X - 1)), dma((Z, X - 1)), dma((Z,)),
            dma((Z, X - 1)), dma((Z, X - 1)), dma((Z,)),
            dma((Z - 1,)), dma((Z - 1,)),
            dma((3,)), dma((3,)), dma((3,)),
        ],
        compiler_params=pltpu.CompilerParams(
            collective_id=0, has_side_effects=True, vmem_limit_bytes=58 << 20
        ),
        name="layer",
    )(
        attn_values, out_proj, residual_in, norm_gain[None], final_gain[None], router.T,
        row_order[None], routes.T, gate_weight[0], up_weight[0], down_weight[0],
    )


def solution(mesh):
    fine = Mesh(mesh.devices.reshape(X, Z, C, -1), ("x", "z", "c", "tp"))
    req = ("x", "z", "c")
    placed = (
        P(req, "tp"),
        P("tp", None),
        P((*req, "tp"), None),
        P(),
        P(),
        P(),
        P(req, None, None),
        P(req, None, None),
        P(req, None, None),
        P((*req, "tp")),
        P((*req, "tp"), None),
    )
    return jax.shard_map(
        shards, mesh=fine, in_specs=placed, out_specs=P((*req, "tp"), None), check_vma=False
    )
```

time: 193 us -> 139 us (0.72); the launches traced: 189 us -> 137 us
  matrix products: 43 us -> 0 us
  local copies, waits for them, and re-layouts: 14.2 us -> 4.24 us
  Pallas kernels: 130 us -> 133 us
  other arithmetic: 2.24 us -> 0 us
    dot_general x5 -> x0, matrix products: 43 us -> none  [the longest x2 27.8 us: shards(): value = jnp.dot(hidden, down, preferred_element_type=F32)]
    unnamed x21 -> x1, local copies, waits for them, and re-layouts: 13 us -> 1.67 us
    pallas_call x2 -> x1, Pallas kernels: 130 us -> 133 us  [shards(): pl.pallas_call(functools.partial(layer, tp), out_shape=jax.ShapeDtypeStru...]
where the time goes in v3:
time: 139 us; the launch traced here: 137 us
  Pallas kernels  133 us (96%)
  local copies, waits for them, and re-layouts  4.24 us (3%)
    pallas_call x1, Pallas kernels, shards(): pl.pallas_call(functools.partial(layer, tp), out_shape=jax.ShapeDtypeStru...  133 us

profile of v3, /device:TPU:10, one launch (start us, length us, event | category | flops | bytes accessed | tf_op | source)
XLA Modules:
  0.0 137.4 jit_solution(3404046031675273957)
XLA Ops:
  0.0 1.3 broadcast_in_dim.9.gain
  1.3 1.3 broadcast_in_dim.10.last_gain
  2.6 133.2 %layer.1 = bf16[64,2048]{1,0:T(8,128)(2,1)} custom-call(bf16[256,512]{1,0:T(8,128)(2,1)} %attn.1, bf16[512,2048]{1,0:T(8,128)(2,1)} %proj.1, bf16[64,2048]{1,0:T(8,128)(2,1)} %resid.1, bf16[1,2048]{1,0:T(2,128)(2,1)} %broadcast_in_dim.9.gain, bf16[1,2048]{1,0:T(2,128)(2,1)} %broadcast_in_dim.10.last_gain, bf16[8,2048]{1,0:T(8,128)(2,1)} %bitcast.9, ...), custom_call_target="tpu_custom_call" | custom-call | tf_op jit(solution)/shard_map/layer/pallas_call | solution.py:297
  135.7 1.7 %copy.13 = bf16[64,2048]{1,0:T(8,128)(2,1)} copy(bf16[64,2048]{1,0:T(8,128)(2,1)} %layer.1) | data formatting | bytes 524288

commit v4 on v3

--- a/solution.py
+++ b/solution.py
@@ -47,8 +47,8 @@
 def layer(
     tp, attn, proj, resid, gain, last_gain, router, order, routes, gate, up, down,
     out,
-    part, inbox, chunk, col, slots, items, partial, got, tail, tails, hidden,
-    gates, ups, downs,
+    values, weights, residual, part, inbox, chunk, col, slots, items, partial, got,
+    tail, tails, hidden, gates, ups, downs, in_sem,
     tp_send, tp_recv, z_send, z_recv, x_send, x_recv, own_sem,
     r_send, r_recv, r_own, t_send, t_recv, w_own, w_send, w_recv,
 ):
@@ -59,9 +59,13 @@
     above, below = {"z": lax.rem(mz + 1, Z)}, {"z": lax.rem(mz + Z - 1, Z)}
     other = {"c": 1 - mc}
     mates = [{"tp": lax.rem(mt + d, tp)} for d in range(1, tp)]
-    column = [{"z": lax.rem(mz + d, Z)} for d in range(1, Z)]
-    ready = greet(mates + column + [other] + [x_peer(mx, d) for d in range(1, X)])
-
+    ready = greet(mates + [above, below, other] + [x_peer(mx, d) for d in range(1, X)])
+
+    first_loads = []
+    for i, (a, b) in enumerate(((attn, values), (proj, weights), (resid, residual))):
+        copy = pltpu.make_async_copy(a, b, in_sem.at[i])
+        copy.start()
+        first_loads.append(copy)
     loads = []
     near, far_side = pl.ds(0, units), pl.ds(units, units)
     for i, (a, b) in enumerate(
@@ -72,13 +76,16 @@
         loads.append(copy)
 
     def term(t):
-        block = attn[pl.ds(pl.multiple_of(t * rows, rows), rows), :]
-        return jnp.dot(block, proj[...], preferred_element_type=F32)
-
+        block = values[pl.ds(pl.multiple_of(t * rows, rows), rows), :]
+        return jnp.dot(block, weights[...], preferred_element_type=F32)
+
+    for copy in first_loads:
+        copy.wait()
     pending = []
-    for d in range(1, tp):
+    turns = sorted(range(1, tp), key=lambda d: -min(d, tp - d))
+    for d in turns:
         part[d - 1] = term(lax.rem(mt + d, tp)).astype(BF16)
-        if d == 1:
+        if not pending:
             ready()
         pending.append(
             remote(part.at[d - 1], inbox.at[d - 1], tp_send.at[d - 1], tp_recv.at[d - 1], mates[d - 1])
@@ -108,16 +115,17 @@
     for k in range(TOP):
         rank = jnp.sum(before * hot[k], axis=1, keepdims=True)
         notes = notes + jnp.where(lane == k, upright(base[k : k + 1, :]) + rank, 0.0)
-
-    for d in range(1, tp):
-        pending[d - 1].wait_recv()
+    notes = jnp.dot(pick_t, notes.astype(BF16), preferred_element_type=F32)
+    hot = [jnp.dot(pick_t, h.astype(BF16), preferred_element_type=F32) for h in hot]
+
+    for copy, d in zip(pending, turns):
+        copy.wait_recv()
         total = total + inbox[d - 1].astype(F32)
-    stream = (resid[...].astype(F32) + total).astype(BF16)
-    normed = root_norm(stream.astype(F32), gain[...]).astype(BF16)
+    stream = (residual[...].astype(F32) + total).astype(BF16)
+    normed = root_norm(stream.astype(F32), gain[...].astype(F32).reshape(1, width)).astype(BF16)
     across = (((0,), (0,)), ((), ()))
-    picked = lax.dot_general(pick_t, normed, across, preferred_element_type=F32).astype(BF16)
     logits = lax.dot_general(
-        picked, router[...], (((1,), (1,)), ((), ())), preferred_element_type=F32
+        normed, router[...], (((1,), (1,)), ((), ())), preferred_element_type=F32
     )
     chosen = [jnp.sum(logits * hot[k], axis=1, keepdims=True) for k in range(TOP)]
     for k in range(TOP):
@@ -125,7 +133,7 @@
         high = w.astype(BF16).astype(F32)
         notes = notes + jnp.where(lane == 2 + k, high, 0.0)
         notes = notes + jnp.where(lane == 4 + k, w - high, 0.0)
-    chunk[:, :width] = picked
+    chunk[:, :width] = normed
     chunk[:, width:] = notes.astype(BF16)
 
     offset = (mz // (Z // 2) * HALF).astype(F32)
@@ -161,7 +169,7 @@
     rising = [remote(chunk, col.at[mz], z_send.at[0, 0], z_recv.at[0, 0], above)]
     falling = [remote(chunk, col.at[mz], z_send.at[1, 0], z_recv.at[1, 0], below)]
     spread(0)
-    soon = {1: (1, 6), 2: (5,), 3: (2, 3)}
+    soon = {1: (1, 6), 2: (), 3: (2, 3)}
     for k in range(1, far):
         low, high = lax.rem(mz + Z - k, Z), lax.rem(mz + k, Z)
         a, b = col.at[low], col.at[high]
@@ -176,6 +184,7 @@
     rising[-1].wait_recv()
     falling[-1].wait_recv()
     spread(4)
+    spread(5)
     spread(7)
 
     for copy in loads:
@@ -222,8 +231,6 @@
         own.start()
         returned[p] = copies, own
 
-    going = []
-
     def combine(p):
         note = block_of(p)[:, width:].astype(F32)
         hit_a, hit_b = note[:, 0:1] - offset == at, note[:, 1:2] - offset == at
@@ -235,13 +242,28 @@
             copy.wait_recv()
         block = got[p].reshape(HALF, width)
         value = jnp.dot(high.astype(BF16), block, preferred_element_type=F32)
-        value = value + jnp.dot(low.astype(BF16), block, preferred_element_type=F32)
-        if p == 0:
-            return value
-        tail[p - 1] = value.astype(BF16)
-        peer = {"z": lax.rem(mz + PLACES[p] + Z, Z)}
-        going.append(
-            remote(tail.at[p - 1], tails.at[p - 1], t_send.at[p - 1], t_recv.at[p - 1], peer)
+        return value + jnp.dot(low.astype(BF16), block, preferred_element_type=F32)
+
+    sums = ([], [])
+
+    def pass_on(way, k, value):
+        if k == 0:
+            kept_rows = (upper, lower)[way]
+            tail[way, k, kept_rows] = value[kept_rows].astype(BF16)
+            a, b = tail.at[way, k, kept_rows], tails.at[way, k, kept_rows]
+        else:
+            sums[way][k - 1].wait_recv()
+            if k == 1:
+                kept_rows = (upper, lower)[way]
+                rest = (lower, upper)[way]
+                added = value[kept_rows] + tails[way, 0, kept_rows].astype(F32)
+                tail[way, k, kept_rows] = added.astype(BF16)
+                tail[way, k, rest] = value[rest].astype(BF16)
+            else:
+                tail[way, k] = (value + tails[way, k - 1].astype(F32)).astype(BF16)
+            a, b = tail.at[way, k], tails.at[way, k]
+        sums[way].append(
+            remote(a, b, t_send.at[way, k], t_recv.at[way, k], (above, below)[way])
         )
 
     experts(0)
@@ -251,22 +273,28 @@
     experts(4)
     give_back(4)
     give_back(5)
-    combine(2)
-    combine(3)
     experts(6)
     for p in (7, 6, 1, 0):
         give_back(p)
-    for p in (4, 5, 7, 6, 1):
-        combine(p)
+    ahead, behind = combine(3), combine(2)
+    value = combine(4)
+    pass_on(0, 0, value)
+    pass_on(1, 0, value)
+    pass_on(0, 1, ahead)
+    pass_on(1, 1, behind)
+    behind, ahead = combine(5), combine(7)
+    pass_on(0, 2, ahead)
+    pass_on(1, 2, behind)
+    ahead, behind = combine(6), combine(1)
+    pass_on(0, 3, ahead)
+    pass_on(1, 3, behind)
     total = combine(0)
-    for i, copy in enumerate(going):
-        copy.wait_recv()
-    for i in range(Z - 1):
-        total = total + tails[i].astype(F32)
-    kept = lax.dot_general(pick_t, stream, across, preferred_element_type=F32)
-    done = root_norm(kept + total, last_gain[...]).astype(BF16)
-    out[...] = jnp.dot(pick_t, done, preferred_element_type=F32).astype(BF16)
-    for copy in pending + rising + falling + swaps + going:
+    for way in (0, 1):
+        sums[way][far - 1].wait_recv()
+        total = total + tails[way, far - 1].astype(F32)
+    last = last_gain[...].astype(F32).reshape(1, width)
+    out[...] = root_norm(stream.astype(F32) + total, last).astype(BF16)
+    for copy in pending + rising + falling + swaps + sums[0] + sums[1]:
         copy.wait_send()
     for group in (sent, returned):
         for copies, _ in group.values():
@@ -297,25 +325,29 @@
     return pl.pallas_call(
         functools.partial(layer, tp),
         out_shape=jax.ShapeDtypeStruct((rows, width), BF16),
-        in_specs=[vmem] * 8 + [hbm] * 3,
+        in_specs=[hbm] * 3 + [vmem] * 5 + [hbm] * 3,
         out_specs=vmem,
         scratch_shapes=[
+            pltpu.VMEM(attn_values.shape, BF16),
+            pltpu.VMEM(out_proj.shape, BF16),
+            pltpu.VMEM((rows, width), BF16),
             pltpu.VMEM((tp - 1, rows, width), BF16),
             pltpu.VMEM((tp - 1, rows, width), BF16),
             pltpu.VMEM((rows, width + META), BF16),
             pltpu.VMEM((Z, rows, width + META), BF16),
             block, block, block, block,
-            pltpu.VMEM((Z - 1, rows, width), BF16),
-            pltpu.VMEM((Z - 1, rows, width), BF16),
+            pltpu.VMEM((2, Z // 2, rows, width), BF16),
+            pltpu.VMEM((2, Z // 2, rows, width), BF16),
             pltpu.VMEM((2 * HALF, 2 * units), BF16),
             pltpu.VMEM((width, 2 * units), BF16),
             pltpu.VMEM((width, 2 * units), BF16),
             pltpu.VMEM((2 * units, width), BF16),
+            dma((3,)),
             dma((tp - 1,)), dma((tp - 1,)),
             dma((2, Z // 2)), dma((2, Z // 2)),
             dma((Z, X - 1)), dma((Z, X - 1)), dma((Z,)),
             dma((Z, X - 1)), dma((Z, X - 1)), dma((Z,)),
-            dma((Z - 1,)), dma((Z - 1,)),
+            dma((2, Z // 2)), dma((2, Z // 2)),
             dma((3,)), dma((3,)), dma((3,)),
         ],
         compiler_params=pltpu.CompilerParams(
@@ -323,7 +355,7 @@
         ),
         name="layer",
     )(
-        attn_values, out_proj, residual_in, norm_gain[None], final_gain[None], router.T,
+        attn_values, out_proj, residual_in, norm_gain, final_gain, router.T,
         row_order[None], routes.T, gate_weight[0], up_weight[0], down_weight[0],
     )
 

time: 139 us -> 131 us (0.942)
  Pallas kernels: 133 us -> 127 us
  local copies, waits for them, and re-layouts: 4.24 us -> 1.67 us
    pallas_call x1, Pallas kernels: 133 us -> 127 us  [shards(): pl.pallas_call(functools.partial(layer, tp), out_shape=jax.ShapeDtypeStru...]
    broadcast_in_dim x2 -> x0, local copies, waits for them, and re-layouts: 2.57 us -> none  [the longest x1 1.29 us: shards(): norm_gain[None]]
where the time goes in v4:
time: 131 us; the launch traced here: 128 us
  Pallas kernels  127 us (97%)
  local copies, waits for them, and re-layouts  1.67 us (1%)
    pallas_call x1, Pallas kernels, shards(): pl.pallas_call(functools.partial(layer, tp), out_shape=jax.ShapeDtypeStru...  127 us

profile of v4, /device:TPU:10, one launch (start us, length us, event | category | flops | bytes accessed | tf_op | source)
XLA Modules:
  0.0 128.2 jit_solution(14951330807056224254)
XLA Ops:
  0.0 126.6 %layer.1 = bf16[64,2048]{1,0:T(8,128)(2,1)} custom-call(bf16[256,512]{1,0:T(8,128)(2,1)} %attn.1, bf16[512,2048]{1,0:T(8,128)(2,1)} %proj.1, bf16[64,2048]{1,0:T(8,128)(2,1)} %resid.1, bf16[2048]{0:T(1024)(128)(2,1)} %gain.1, bf16[2048]{0:T(1024)(128)(2,1)} %last_gain.1, bf16[8,2048]{1,0:T(8,128)(2,1)} %bitcast.9, s32[1,64]{1,0:T(1,128)} %bitcast.11, ...), custom_call_target="tpu_custom_call" | custom-call | tf_op jit(solution)/shard_map/layer/pallas_call | solution.py:325
  126.6 1.7 %copy.13 = bf16[64,2048]{1,0:T(8,128)(2,1)} copy(bf16[64,2048]{1,0:T(8,128)(2,1)} %layer.1) | data formatting | bytes 524288
